TPU v7x, 32 devices: a whole 2x2x4 slice. The times are simulated.
32 devices in a mesh: gx: 4 (over z), gy: 8 (over y, x, core).
Axes of the slice: x: 2, y: 2, z: 4, core: 2. Of those that a mesh axis runs over, the one named last changes fastest.
Arguments:
- data: bfloat16 [128, 512, 1024], P(None, 'gx', 'gy')
- inv_scale: float32 [128], replicated, may hold values from 0.1 to 1
- start: float32 [128, 32], replicated, may hold values from -6 to 6
- rank: int32 [1], replicated, may hold values from 24 to 32
Outputs:
- core: bfloat16 [32, 512, 1024], P(None, 'gx', 'gy')
- factor: float32 [128, 32], replicated
Inputs may be any that keep to these rules, and one draw needn't show every extreme that they name: rank[0] is the number of leading columns of the factor that are kept.
All inputs are finite; a program needn't handle non-finite values.
Results may differ from a plain program's by a relative error of at most 0.0044.
Values sent between devices are 32-bit elements; how exact they have to be, the bound alone decides.
A program may use at most 64 MiB of HBM per device.

v0:
```python
import jax
import jax.numpy as jnp
from jax import lax
from jax.sharding import PartitionSpec as P

ITERS = 4


def body(data, inv_scale, start, rank):
    variables = data.shape[0]
    columns = start.shape[1]
    flat = data.reshape(variables, -1)
    local_gram = lax.dot_general(
        flat, flat, (((1,), (1,)), ((), ())), preferred_element_type=jnp.float32
    )
    gram = lax.psum(local_gram, ("gx", "gy"))
    weighted = inv_scale[:, None] * gram * inv_scale[None, :]
    basis = start
    for turn in range(ITERS):
        image = jnp.dot(weighted, basis, precision=lax.Precision.HIGHEST)
        inner = jnp.dot(image.T, image, precision=lax.Precision.HIGHEST)
        lower = jnp.linalg.cholesky(inner)
        basis = lax.linalg.triangular_solve(
            lower, image, left_side=False, lower=True, transpose_a=True
        )
    keep = (jnp.arange(columns, dtype=jnp.int32) < rank[0]).astype(jnp.float32)
    factor = basis * keep[None, :]
    scaled_factor = (inv_scale[:, None] * factor).astype(jnp.bfloat16)
    product = lax.dot_general(
        scaled_factor, flat, (((0,), (0,)), ((), ())), preferred_element_type=jnp.float32
    )
    core = product.astype(jnp.bfloat16).reshape(columns, data.shape[1], data.shape[2])
    return (core, factor)


def solution(mesh):
    in_specs = (P(None, "gx", "gy"), P(), P(), P())
    out_specs = (P(None, "gx", "gy"), P())
    return jax.shard_map(body, mesh=mesh, in_specs=in_specs, out_specs=out_specs, check_vma=False)
```

profile of v0, /device:TPU:0, one launch (start us, length us, event | category | flops | bytes accessed | tf_op | source)
XLA Modules:
  0.0 184.4 jit_solution(14243155040835074727)
XLA Ops:
  7.2 8.8 %fusion.7 = f32[128,128]{1,0:T(8,128)} fusion(bf16[128,128,128]{2,1,0:T(8,128)(2,1)} %param.7), kind=kOutput, calls=%fused_computation.6 | convolution fusion | flops 536870912 | bytes 4259840 | tf_op jit(solution)/shard_map/dot_general | solution.py:13
  16.7 121.6 %all-reduce.2.cloned.1.call-done = f32[128,128]{1,0:T(8,128)} async-done(((f32[128,128]{1,0:T(8,128)}), f32[128,128]{1,0:T(8,128)}) %all-reduce.2.cloned.1.call-update) | async-done | bytes 65552 | tf_op jit(solution)/shard_map/psum | solution.py:16
  138.3 1.1 fusion.14
  139.7 2.9 %cholesky.74 = f32[32,32]{1,0:T(8,128)S(1)} custom-call(f32[32,32]{1,0:T(8,128)S(1)} %fusion.34), custom_call_target="Cholesky" | custom-call | tf_op jit(solution)/shard_map/jit(cholesky)/cholesky | solution.py:22
  142.6 0.6 compare_reduce_fusion.3
  143.3 0.7 fusion.23
  143.9 2.4 %custom-call.8 = f32[1,32,32]{1,2,0:T(8,128)S(1)} custom-call(f32[1,32,32]{2,1,0:T(8,128)S(1)} %fusion.23), custom_call_target="InvertDiagBlocksLowerTriangular" | custom-call | tf_op jit(solution)/shard_map/triangular_solve/custom-call.0 | solution.py:23
  146.6 1.1 fusion.13
  148.0 2.9 %cholesky.85 = f32[32,32]{1,0:T(8,128)S(1)} custom-call(f32[32,32]{1,0:T(8,128)S(1)} %fusion.32), custom_call_target="Cholesky" | custom-call | tf_op jit(solution)/shard_map/jit(cholesky)/cholesky | solution.py:22
  150.9 0.6 compare_reduce_fusion.2
  151.6 0.7 fusion.24
  152.2 2.4 %custom-call.9 = f32[1,32,32]{1,2,0:T(8,128)S(1)} custom-call(f32[1,32,32]{2,1,0:T(8,128)S(1)} %fusion.24), custom_call_target="InvertDiagBlocksLowerTriangular" | custom-call | tf_op jit(solution)/shard_map/triangular_solve/custom-call.0 | solution.py:23
  154.9 1.1 fusion.12
  156.3 2.9 %cholesky.96 = f32[32,32]{1,0:T(8,128)S(1)} custom-call(f32[32,32]{1,0:T(8,128)S(1)} %fusion.30), custom_call_target="Cholesky" | custom-call | tf_op jit(solution)/shard_map/jit(cholesky)/cholesky | solution.py:22
  159.3 0.6 compare_reduce_fusion.1
  159.9 0.7 fusion.25
  160.6 2.4 %custom-call.10 = f32[1,32,32]{1,2,0:T(8,128)S(1)} custom-call(f32[1,32,32]{2,1,0:T(8,128)S(1)} %fusion.25), custom_call_target="InvertDiagBlocksLowerTriangular" | custom-call | tf_op jit(solution)/shard_map/triangular_solve/custom-call.0 | solution.py:23
  163.2 1.1 fusion.11
  164.6 2.9 %cholesky.107 = f32[32,32]{1,0:T(8,128)S(1)} custom-call(f32[32,32]{1,0:T(8,128)S(1)} %fusion.28), custom_call_target="Cholesky" | custom-call | tf_op jit(solution)/shard_map/jit(cholesky)/cholesky | solution.py:22
  167.6 0.6 compare_reduce_fusion
  168.2 0.7 fusion.26
  168.9 2.4 %custom-call.11 = f32[1,32,32]{1,2,0:T(8,128)S(1)} custom-call(f32[1,32,32]{2,1,0:T(8,128)S(1)} %fusion.26), custom_call_target="InvertDiagBlocksLowerTriangular" | custom-call | tf_op jit(solution)/shard_map/triangular_solve/custom-call.0 | solution.py:23
  171.6 4.8 %fusion.4 = bf16[4,8,128,128]{3,1,2,0:T(8,128)(2,1)S(1)} fusion(bf16[16,8,128,128]{3,2,1,0:T(8,128)(2,1)} %bitcast.75, f32[128,32]{0,1:T(8,128)S(1)} %fusion.10, f32[128]{0:T(128)S(1)} %copy-done.1), kind=kOutput, calls=%fused_computation.5 | convolution fusion | flops 134750208 | bytes 5259776 | tf_op jit(solution)/shard_map/dot_general | solution.py:29
  176.4 1.2 copy.13
  (29 shorter events, 2.1 us)
Async XLA Ops:
  7.2 131.1 %copy-start = (f32[128,32]{0,1:T(8,128)S(1)}, f32[128,32]{0,1:T(8,128)}, u32[]{:S(2)}) copy-start(f32[128,32]{0,1:T(8,128)} %param.9) | copy-start | bytes 49156
  7.2 131.1 %copy-start.1 = (f32[128]{0:T(128)S(1)}, f32[128]{0:T(128)}, u32[]{:S(2)}) copy-start(f32[128]{0:T(128)} %param.8) | copy-start | bytes 1540
  7.2 131.1 %all-reduce.2.cloned.1.call-start = ((), (), s32[]{:S(2)}) async-start(), calls=%async_computation | async-start | bytes 131072 | tf_op jit(solution)/shard_map/psum | solution.py:16
  171.6 6.0 %copy-start.2 = (f32[128,32]{0,1:T(8,128)}, f32[128,32]{0,1:T(8,128)S(1)}, u32[]{:S(2)}) copy-start(f32[128,32]{0,1:T(8,128)S(1)} %fusion.10) | copy-start | bytes 49156
Sparse Core Ops, SparseCore 0:
  16.1 122.1 all-reduce.1
where the time goes:
time: 186 us; the launch traced here: 184 us
  waiting for transfers between devices  122 us (66%)
  other arithmetic  26.8 us (14%)
  matrix products  19.6 us (11%)
  between operations  14.9 us (8%)
    psum x1, waiting for transfers between devices, body(): gram = lax.psum(local_gram, ('gx', 'gy'))  122 us
    another operation x12, other arithmetic, body(): lower = jnp.linalg.cholesky(inner)  14.4 us
    another operation x8, other arithmetic, body(): lax.linalg.triangular_solve(lower, image, left_side=False, lower=True, tr...  12.3 us
    dot_general x1, matrix products, body(): lax.dot_general(flat, flat, (((1,), (1,)), ((), ())), preferred_element_t...  8.76 us
    dot_general x1, matrix products, body(): lax.dot_general(scaled_factor, flat, (((0,), (0,)), ((), ())), preferred_...  4.81 us
    dot_general x4, matrix products, body(): image = jnp.dot(weighted, basis, precision=lax.Precision.HIGHEST)  4.42 us
  transfers between devices with their start and end apart: 1, of which 1 were waited for; matrix products, arithmetic and copies ran while one was open for 0% of the time, Pallas kernels for 0%

commit v1 on v0

v1 whole, which is shorter than its diff:
```python
import functools

import jax
import jax.numpy as jnp
from jax import lax
from jax.experimental import pallas as pl
from jax.experimental.pallas import tpu as pltpu
from jax.sharding import PartitionSpec as P

ITERS = 4
GROUP = 16
MESH = pl.DeviceIdType.MESH
HIGHEST = lax.Precision.HIGHEST
NT = (((1,), (1,)), ((), ()))


def gram_kernel(nx, ny, data_hbm, out_ref, slab, part, recv, mid, full,
                load_sem, send1, recv1, send2, recv2, send3, recv3):
    variables, rows, columns = data_hbm.shape
    chunks = rows // GROUP
    height = variables // ny
    me_x = lax.axis_index("gx")
    me_y = lax.axis_index("gy")

    def load(c):
        return pltpu.make_async_copy(
            data_hbm.at[:, pl.ds(c * GROUP, GROUP), :], slab.at[c], load_sem.at[c])

    for c in range(chunks):
        load(c).start()
    barrier = pltpu.get_barrier_semaphore()
    for p in range(1, ny):
        pl.semaphore_signal(barrier, inc=1, device_id=(me_x, lax.rem(me_y + p, ny)), device_id_type=MESH)
    for p in range(1, nx):
        pl.semaphore_signal(barrier, inc=1, device_id=(lax.rem(me_x + p, nx), me_y), device_id_type=MESH)

    gram = jnp.zeros((variables, variables), jnp.float32)
    for c in range(chunks):
        load(c).wait()
        turned = jnp.swapaxes(slab[c], 0, 1)
        for i in range(0, GROUP, 2):
            pair = jnp.concatenate([turned[i], turned[i + 1]], axis=1)
            gram = gram + lax.dot_general(pair, pair, NT, preferred_element_type=jnp.float32)
    for p in range(ny):
        part[p] = gram[p * height:(p + 1) * height, :]
    pl.semaphore_wait(barrier, nx + ny - 2)

    def scatter(p):
        dst = lax.rem(me_y + p, ny)
        return pltpu.make_async_remote_copy(
            src_ref=part.at[dst], dst_ref=recv.at[p - 1],
            send_sem=send1.at[p - 1], recv_sem=recv1.at[p - 1],
            device_id=(me_x, dst), device_id_type=MESH)

    for p in range(1, ny):
        scatter(p).start()
    total = part[me_y]
    for p in range(1, ny):
        scatter(p).wait_recv()
        total = total + recv[p - 1]
    mid[me_x] = total

    def exchange(p):
        return pltpu.make_async_remote_copy(
            src_ref=mid.at[me_x], dst_ref=mid.at[me_x],
            send_sem=send2.at[p - 1], recv_sem=recv2.at[p - 1],
            device_id=(lax.rem(me_x + p, nx), me_y), device_id_type=MESH)

    for p in range(1, nx):
        exchange(p).start()
    for p in range(1, nx):
        exchange(p).wait_recv()
    total = mid[0]
    for s in range(1, nx):
        total = total + mid[s]
    full[me_y] = total

    def gather(p):
        return pltpu.make_async_remote_copy(
            src_ref=full.at[me_y], dst_ref=full.at[me_y],
            send_sem=send3.at[p - 1], recv_sem=recv3.at[p - 1],
            device_id=(me_x, lax.rem(me_y + p, ny)), device_id_type=MESH)

    for p in range(1, ny):
        gather(p).start()
    for p in range(1, ny):
        gather(p).wait_recv()
    for p in range(ny):
        out_ref[p * height:(p + 1) * height, :] = full[p]
    for p in range(1, ny):
        scatter(p).wait_send()
        gather(p).wait_send()
    for p in range(1, nx):
        exchange(p).wait_send()


def summed_gram(mesh, data):
    nx, ny = mesh.shape["gx"], mesh.shape["gy"]
    variables, rows, columns = data.shape
    chunks = rows // GROUP
    height = variables // ny
    dma = pltpu.SemaphoreType.DMA
    return pl.pallas_call(
        functools.partial(gram_kernel, nx, ny),
        out_shape=jax.ShapeDtypeStruct((variables, variables), jnp.float32),
        in_specs=[pl.BlockSpec(memory_space=pl.ANY)],
        out_specs=pl.BlockSpec(memory_space=pltpu.VMEM),
        scratch_shapes=[
            pltpu.VMEM((chunks, variables, GROUP, columns), data.dtype),
            pltpu.VMEM((ny, height, variables), jnp.float32),
            pltpu.VMEM((ny - 1, height, variables), jnp.float32),
            pltpu.VMEM((nx, height, variables), jnp.float32),
            pltpu.VMEM((ny, height, variables), jnp.float32),
            dma((chunks,)),
            dma((ny - 1,)), dma((ny - 1,)),
            dma((nx - 1,)), dma((nx - 1,)),
            dma((ny - 1,)), dma((ny - 1,)),
        ],
        compiler_params=pltpu.CompilerParams(collective_id=0, has_side_effects=True),
        name="gram",
    )(data)


def orthonormal(image):
    count, lanes = image.shape
    inner = lax.dot_general(image, image, NT, precision=HIGHEST, preferred_element_type=jnp.float32)
    blocks = count // 8
    sub = lax.broadcasted_iota(jnp.int32, (8, lanes), 0)
    cols = []
    for k in range(count):
        wide = jnp.broadcast_to(inner[:, k:k + 1], (count, lanes))
        cols.append([wide[8 * b:8 * b + 8] for b in range(blocks)])
    img = [image[8 * b:8 * b + 8] for b in range(blocks)]

    def spread(block, row):
        return jnp.broadcast_to(block[row:row + 1, :], (8, lanes))

    for k in range(count):
        kb, kr = divmod(k, 8)
        col = cols[k]
        pivot = spread(col[kb], kr)
        inverse = 1.0 / pivot
        scale = lax.rsqrt(pivot)
        row = spread(img[kb], kr)
        low = {}
        for b in range(kb, blocks):
            value = col[b] * inverse
            if b == kb:
                value = jnp.where(sub > kr, value, 0.0)
            low[b] = value
        for j in range(k + 1, count):
            jb, jr = divmod(j, 8)
            factor = spread(col[jb], jr)
            for b in range(jb, blocks):
                cols[j][b] = cols[j][b] - low[b] * factor
        for b in range(kb, blocks):
            img[b] = img[b] - low[b] * row
        img[kb] = img[kb] * jnp.where(sub == kr, scale, 1.0)
    return jnp.concatenate(img, axis=0)


def project_kernel(rank_ref, gram_ref, scale_ref, start_ref, data_hbm, core_hbm, factor_ref,
                   slab, done, load_sem, store_sem):
    variables, rows, columns = data_hbm.shape
    count = start_ref.shape[1]
    chunks = rows // GROUP

    def load(c):
        return pltpu.make_async_copy(
            data_hbm.at[:, pl.ds(c * GROUP, GROUP), :], slab.at[c], load_sem.at[c])

    def store(c):
        return pltpu.make_async_copy(
            done.at[c], core_hbm.at[:, pl.ds(c * GROUP, GROUP), :], store_sem.at[c])

    for c in range(chunks):
        load(c).start()
    scale_row = jnp.broadcast_to(scale_ref[...], (variables, variables))
    weighted = scale_row.T * gram_ref[...] * scale_row
    basis = start_ref[...].T

    def turn(_, basis):
        image = jnp.dot(basis, weighted, precision=HIGHEST, preferred_element_type=jnp.float32)
        return orthonormal(image)

    basis = lax.fori_loop(0, ITERS, turn, basis)
    kept = lax.broadcasted_iota(jnp.int32, basis.shape, 0) < rank_ref[0]
    factor = jnp.where(kept, basis, 0.0)
    factor_ref[...] = factor.T
    scaled = (scale_row[:count] * factor).astype(jnp.bfloat16)

    tall, long = count * GROUP, variables * GROUP
    pick_k = (lax.broadcasted_iota(jnp.int32, (tall, count), 0) // GROUP
              == lax.broadcasted_iota(jnp.int32, (tall, count), 1)).astype(jnp.bfloat16)
    pick_v = (lax.broadcasted_iota(jnp.int32, (variables, long), 1) // GROUP
              == lax.broadcasted_iota(jnp.int32, (variables, long), 0)).astype(jnp.bfloat16)
    repeated = jnp.dot(pick_k, scaled, preferred_element_type=jnp.float32).astype(jnp.bfloat16)
    spread = jnp.dot(repeated, pick_v, preferred_element_type=jnp.float32)
    same = (lax.broadcasted_iota(jnp.int32, (tall, long), 0) % GROUP
            == lax.broadcasted_iota(jnp.int32, (tall, long), 1) % GROUP)
    wide = jnp.where(same, spread, 0.0).astype(jnp.bfloat16)
    for c in range(0, chunks, 2):
        load(c).wait()
        load(c + 1).wait()
        pair = jnp.concatenate([slab[c].reshape(long, columns), slab[c + 1].reshape(long, columns)], axis=1)
        product = jnp.dot(wide, pair, preferred_element_type=jnp.float32).astype(jnp.bfloat16)
        for h in range(2):
            done[c + h] = product[:, h * columns:(h + 1) * columns].reshape(count, GROUP, columns)
            store(c + h).start()
    for c in range(chunks):
        store(c).wait()


def project(rank, gram, inv_scale, start, data):
    variables, rows, columns = data.shape
    count = start.shape[1]
    chunks = rows // GROUP
    vmem = pl.BlockSpec(memory_space=pltpu.VMEM)
    return pl.pallas_call(
        project_kernel,
        out_shape=(
            jax.ShapeDtypeStruct((count, rows, columns), data.dtype),
            jax.ShapeDtypeStruct((variables, count), jnp.float32),
        ),
        in_specs=[pl.BlockSpec(memory_space=pltpu.SMEM), vmem, vmem, vmem,
                  pl.BlockSpec(memory_space=pl.ANY)],
        out_specs=(pl.BlockSpec(memory_space=pl.ANY), vmem),
        scratch_shapes=[
            pltpu.VMEM((chunks, variables, GROUP, columns), data.dtype),
            pltpu.VMEM((chunks, count, GROUP, columns), data.dtype),
            pltpu.SemaphoreType.DMA((chunks,)),
            pltpu.SemaphoreType.DMA((chunks,)),
        ],
        name="project",
    )(rank, gram, inv_scale.reshape(1, variables), start, data)


def solution(mesh):
    def body(data, inv_scale, start, rank):
        gram = summed_gram(mesh, data)
        return project(rank, gram, inv_scale, start, data)

    in_specs = (P(None, "gx", "gy"), P(), P(), P())
    out_specs = (P(None, "gx", "gy"), P())
    return jax.shard_map(body, mesh=mesh, in_specs=in_specs, out_specs=out_specs, check_vma=False)
```

time: 186 us -> 34.4 us (0.18)
  waiting for transfers between devices: 122 us -> 0 us
  Pallas kernels: 0 us -> 29.9 us
  other arithmetic: 26.8 us -> 0 us
  matrix products: 19.6 us -> 0 us
  between operations: 14.9 us -> 1.29 us
    psum x1 -> x0, waiting for transfers between devices: 122 us -> none  [body(): gram = lax.psum(local_gram, ('gx', 'gy'))]
    pallas_call x0 -> x2, Pallas kernels: none -> 29.9 us  [the longest x1 18.2 us: summed_gram(): pl.pallas_call(functools.partial(gram_kernel, nx, ny), out_shape=jax.Shap...]
    another operation x20 -> x0, other arithmetic: 26.7 us -> none  [the longest x12 14.4 us: body(): lower = jnp.linalg.cholesky(inner)]
    dot_general x10 -> x0, matrix products: 18.7 us -> none  [the longest x1 8.76 us: body(): lax.dot_general(flat, flat, (((1,), (1,)), ((), ())), preferred_element_t...]
  transfers between devices with their start and end apart: 1 -> 0, of which waited for: 1 -> 0; matrix products, arithmetic and copies ran while one was open for 0% -> 0% of each run, Pallas kernels for 0% -> 0%
where the time goes in v1:
time: 34.4 us; the launch traced here: 34.1 us
  Pallas kernels  29.9 us (87%)
  local copies, waits for them, and re-layouts  2.96 us (9%)
  between operations  1.29 us (4%)
    pallas_call x1, Pallas kernels, summed_gram(): pl.pallas_call(functools.partial(gram_kernel, nx, ny), out_shape=jax.Shap...  18.2 us
    pallas_call x1, Pallas kernels, project(): pl.pallas_call(project_kernel, out_shape=(jax.ShapeDtypeStruct((count, ro...  11.7 us
    pallas_call x1, local copies, waits for them, and re-layouts, project(): pl.pallas_call(project_kernel, out_shape=(jax.ShapeDtypeStruct((count, ro...  1.52 us
    unnamed x1, local copies, waits for them, and re-layouts  1.44 us

profile of v1, /device:TPU:0, one launch (start us, length us, event | category | flops | bytes accessed | tf_op | source)
XLA Modules:
  0.0 34.1 jit_solution(13243135683652526090)
XLA Ops:
  1.3 1.4 %copy.6.start_ref = f32[128,32]{1,0:T(8,128)} copy(f32[128,32]{0,1:T(8,128)} %param.6) | data formatting | bytes 32768 | tf_op args[2]
  2.7 18.2 %gram.1.gram_ref = f32[128,128]{1,0:T(8,128)} custom-call(bf16[128,128,128]{2,1,0:T(8,128)(2,1)} %data_hbm.3), custom_call_target="tpu_custom_call" | custom-call | tf_op jit(solution)/shard_map/gram/pallas_call | solution.py:103
  20.9 11.7 %project.1 = (bf16[32,128,128]{2,1,0:T(8,128)(2,1)}, f32[128,32]{1,0:T(8,128)}) custom-call(s32[1]{0:T(128)S(6)} %copy.8.rank_ref, f32[128,128]{1,0:T(8,128)} %gram.1.gram_ref, f32[1,128]{1,0:T(1,128)} %bitcast.1, f32[128,32]{1,0:T(8,128)} %copy.6.start_ref, bf16[128,128,128]{2,1,0:T(8,128)(2,1)} %data_hbm.3), custom_call_target="tpu_custom_call" | custom-call | tf_op jit(solution)/shard_map/project/pallas_call | solution.py:219
  32.6 1.5 %copy.7 = f32[128,32]{0,1:T(8,128)} copy(f32[128,32]{1,0:T(8,128)} %get-tuple-element.3) | data formatting | bytes 32768 | tf_op jit(solution)/shard_map/project/pallas_call | solution.py:219

commit v2 on v1

--- a/solution.py
+++ b/solution.py
@@ -14,8 +14,8 @@
 NT = (((1,), (1,)), ((), ()))
 
 
-def gram_kernel(nx, ny, data_hbm, out_ref, slab, part, recv, mid, full,
-                load_sem, send1, recv1, send2, recv2, send3, recv3):
+def gram_kernel(nx, ny, data_hbm, out_ref, turned_hbm, slab, turned, part, recv, mid, full,
+                load_sem, keep_sem, send1, recv1, send2, recv2, send3, recv3):
     variables, rows, columns = data_hbm.shape
     chunks = rows // GROUP
     height = variables // ny
@@ -26,6 +26,10 @@
         return pltpu.make_async_copy(
             data_hbm.at[:, pl.ds(c * GROUP, GROUP), :], slab.at[c], load_sem.at[c])
 
+    def keep(c):
+        return pltpu.make_async_copy(
+            turned.at[c], turned_hbm.at[pl.ds(c * GROUP, GROUP)], keep_sem.at[c])
+
     for c in range(chunks):
         load(c).start()
     barrier = pltpu.get_barrier_semaphore()
@@ -37,9 +41,10 @@
     gram = jnp.zeros((variables, variables), jnp.float32)
     for c in range(chunks):
         load(c).wait()
-        turned = jnp.swapaxes(slab[c], 0, 1)
+        block = jnp.swapaxes(slab[c], 0, 1)
+        turned[c] = block
         for i in range(0, GROUP, 2):
-            pair = jnp.concatenate([turned[i], turned[i + 1]], axis=1)
+            pair = jnp.concatenate([block[i], block[i + 1]], axis=1)
             gram = gram + lax.dot_general(pair, pair, NT, preferred_element_type=jnp.float32)
     for p in range(ny):
         part[p] = gram[p * height:(p + 1) * height, :]
@@ -54,6 +59,8 @@
 
     for p in range(1, ny):
         scatter(p).start()
+    for c in range(chunks):
+        keep(c).start()
     total = part[me_y]
     for p in range(1, ny):
         scatter(p).wait_recv()
@@ -92,6 +99,8 @@
         gather(p).wait_send()
     for p in range(1, nx):
         exchange(p).wait_send()
+    for c in range(chunks):
+        keep(c).wait()
 
 
 def summed_gram(mesh, data):
@@ -102,16 +111,20 @@
     dma = pltpu.SemaphoreType.DMA
     return pl.pallas_call(
         functools.partial(gram_kernel, nx, ny),
-        out_shape=jax.ShapeDtypeStruct((variables, variables), jnp.float32),
+        out_shape=(
+            jax.ShapeDtypeStruct((variables, variables), jnp.float32),
+            jax.ShapeDtypeStruct((rows, variables, columns), data.dtype),
+        ),
         in_specs=[pl.BlockSpec(memory_space=pl.ANY)],
-        out_specs=pl.BlockSpec(memory_space=pltpu.VMEM),
+        out_specs=(pl.BlockSpec(memory_space=pltpu.VMEM), pl.BlockSpec(memory_space=pl.ANY)),
         scratch_shapes=[
             pltpu.VMEM((chunks, variables, GROUP, columns), data.dtype),
+            pltpu.VMEM((chunks, GROUP, variables, columns), data.dtype),
             pltpu.VMEM((ny, height, variables), jnp.float32),
             pltpu.VMEM((ny - 1, height, variables), jnp.float32),
             pltpu.VMEM((nx, height, variables), jnp.float32),
             pltpu.VMEM((ny, height, variables), jnp.float32),
-            dma((chunks,)),
+            dma((chunks,)), dma((chunks,)),
             dma((ny - 1,)), dma((ny - 1,)),
             dma((nx - 1,)), dma((nx - 1,)),
             dma((ny - 1,)), dma((ny - 1,)),
@@ -159,15 +172,15 @@
     return jnp.concatenate(img, axis=0)
 
 
-def project_kernel(rank_ref, gram_ref, scale_ref, start_ref, data_hbm, core_hbm, factor_ref,
+def project_kernel(rank_ref, gram_ref, scale_ref, start_ref, turned_hbm, core_hbm, factor_ref,
                    slab, done, load_sem, store_sem):
-    variables, rows, columns = data_hbm.shape
-    count = start_ref.shape[1]
+    rows, variables, columns = turned_hbm.shape
+    count = start_ref.shape[0]
     chunks = rows // GROUP
 
     def load(c):
         return pltpu.make_async_copy(
-            data_hbm.at[:, pl.ds(c * GROUP, GROUP), :], slab.at[c], load_sem.at[c])
+            turned_hbm.at[pl.ds(c * GROUP, GROUP)], slab.at[c], load_sem.at[c])
 
     def store(c):
         return pltpu.make_async_copy(
@@ -177,7 +190,7 @@
         load(c).start()
     scale_row = jnp.broadcast_to(scale_ref[...], (variables, variables))
     weighted = scale_row.T * gram_ref[...] * scale_row
-    basis = start_ref[...].T
+    basis = start_ref[...]
 
     def turn(_, basis):
         image = jnp.dot(basis, weighted, precision=HIGHEST, preferred_element_type=jnp.float32)
@@ -186,59 +199,51 @@
     basis = lax.fori_loop(0, ITERS, turn, basis)
     kept = lax.broadcasted_iota(jnp.int32, basis.shape, 0) < rank_ref[0]
     factor = jnp.where(kept, basis, 0.0)
-    factor_ref[...] = factor.T
+    factor_ref[...] = factor
     scaled = (scale_row[:count] * factor).astype(jnp.bfloat16)
 
-    tall, long = count * GROUP, variables * GROUP
-    pick_k = (lax.broadcasted_iota(jnp.int32, (tall, count), 0) // GROUP
-              == lax.broadcasted_iota(jnp.int32, (tall, count), 1)).astype(jnp.bfloat16)
-    pick_v = (lax.broadcasted_iota(jnp.int32, (variables, long), 1) // GROUP
-              == lax.broadcasted_iota(jnp.int32, (variables, long), 0)).astype(jnp.bfloat16)
-    repeated = jnp.dot(pick_k, scaled, preferred_element_type=jnp.float32).astype(jnp.bfloat16)
-    spread = jnp.dot(repeated, pick_v, preferred_element_type=jnp.float32)
-    same = (lax.broadcasted_iota(jnp.int32, (tall, long), 0) % GROUP
-            == lax.broadcasted_iota(jnp.int32, (tall, long), 1) % GROUP)
-    wide = jnp.where(same, spread, 0.0).astype(jnp.bfloat16)
-    for c in range(0, chunks, 2):
+    for c in range(chunks):
         load(c).wait()
-        load(c + 1).wait()
-        pair = jnp.concatenate([slab[c].reshape(long, columns), slab[c + 1].reshape(long, columns)], axis=1)
-        product = jnp.dot(wide, pair, preferred_element_type=jnp.float32).astype(jnp.bfloat16)
-        for h in range(2):
-            done[c + h] = product[:, h * columns:(h + 1) * columns].reshape(count, GROUP, columns)
-            store(c + h).start()
+        planes = []
+        for i in range(0, GROUP, 2):
+            pair = jnp.concatenate([slab[c, i], slab[c, i + 1]], axis=1)
+            product = jnp.dot(scaled, pair, preferred_element_type=jnp.float32).astype(jnp.bfloat16)
+            planes += [product[:, :columns], product[:, columns:]]
+        done[c] = jnp.swapaxes(jnp.stack(planes), 0, 1)
+        store(c).start()
     for c in range(chunks):
         store(c).wait()
 
 
 def project(rank, gram, inv_scale, start, data):
-    variables, rows, columns = data.shape
+    rows, variables, columns = data.shape
     count = start.shape[1]
     chunks = rows // GROUP
     vmem = pl.BlockSpec(memory_space=pltpu.VMEM)
-    return pl.pallas_call(
+    core, turned = pl.pallas_call(
         project_kernel,
         out_shape=(
             jax.ShapeDtypeStruct((count, rows, columns), data.dtype),
-            jax.ShapeDtypeStruct((variables, count), jnp.float32),
+            jax.ShapeDtypeStruct((count, variables), jnp.float32),
         ),
         in_specs=[pl.BlockSpec(memory_space=pltpu.SMEM), vmem, vmem, vmem,
                   pl.BlockSpec(memory_space=pl.ANY)],
         out_specs=(pl.BlockSpec(memory_space=pl.ANY), vmem),
         scratch_shapes=[
-            pltpu.VMEM((chunks, variables, GROUP, columns), data.dtype),
+            pltpu.VMEM((chunks, GROUP, variables, columns), data.dtype),
             pltpu.VMEM((chunks, count, GROUP, columns), data.dtype),
             pltpu.SemaphoreType.DMA((chunks,)),
             pltpu.SemaphoreType.DMA((chunks,)),
         ],
         name="project",
-    )(rank, gram, inv_scale.reshape(1, variables), start, data)
+    )(rank, gram, inv_scale.reshape(1, variables), start.T, data)
+    return core, turned.T
 
 
 def solution(mesh):
     def body(data, inv_scale, start, rank):
-        gram = summed_gram(mesh, data)
-        return project(rank, gram, inv_scale, start, data)
+        gram, turned = summed_gram(mesh, data)
+        return project(rank, gram, inv_scale, start, turned)
 
     in_specs = (P(None, "gx", "gy"), P(), P(), P())
     out_specs = (P(None, "gx", "gy"), P())

time: 34.4 us -> 27.6 us (0.80)
  Pallas kernels: 29.9 us -> 26.1 us
  local copies, waits for them, and re-layouts: 2.96 us -> 0 us
    pallas_call x1, Pallas kernels: 11.7 us -> 7.75 us  [project(): pl.pallas_call(project_kernel, out_shape=(jax.ShapeDtypeStruct((count, ro...]
    pallas_call x1 -> x0, local copies, waits for them, and re-layouts: 1.52 us -> none  [project(): pl.pallas_call(project_kernel, out_shape=(jax.ShapeDtypeStruct((count, ro...]
    unnamed x1 -> x0, local copies, waits for them, and re-layouts: 1.44 us -> none
where the time goes in v2:
time: 27.6 us; the launch traced here: 27.4 us
  Pallas kernels  26.1 us (95%)
  between operations  1.28 us (5%)
    pallas_call x1, Pallas kernels, summed_gram(): pl.pallas_call(functools.partial(gram_kernel, nx, ny), out_shape=(jax.Sha...  18.4 us
    pallas_call x1, Pallas kernels, project(): pl.pallas_call(project_kernel, out_shape=(jax.ShapeDtypeStruct((count, ro...  7.75 us

profile of v2, /device:TPU:0, one launch (start us, length us, event | category | flops | bytes accessed | tf_op | source)
XLA Modules:
  0.0 27.4 jit_solution(4388553761222919621)
XLA Ops:
  1.3 18.4 %gram.1 = (f32[128,128]{1,0:T(8,128)}, bf16[128,128,128]{2,1,0:T(8,128)(2,1)}) custom-call(bf16[128,128,128]{2,1,0:T(8,128)(2,1)} %data_hbm.1), custom_call_target="tpu_custom_call" | custom-call | tf_op jit(solution)/shard_map/gram/pallas_call | solution.py:112
  19.6 7.7 %project.1 = (bf16[32,128,128]{2,1,0:T(8,128)(2,1)}, f32[32,128]{1,0:T(8,128)}) custom-call(s32[1]{0:T(128)S(6)} %copy.6.rank_ref, f32[128,128]{1,0:T(8,128)} %get-tuple-element.6.gram_ref, f32[1,128]{1,0:T(1,128)} %bitcast.4, f32[32,128]{1,0:T(8,128)} %bitcast.3, bf16[128,128,128]{2,1,0:T(8,128)(2,1)} %get-tuple-element.7.turned_hbm), custom_call_target="tpu_custom_call" | custom-call | tf_op jit(solution)/shard_map/project/pallas_call | solution.py:223

commit v3 on v2

--- a/solution.py
+++ b/solution.py
@@ -59,8 +59,6 @@
 
     for p in range(1, ny):
         scatter(p).start()
-    for c in range(chunks):
-        keep(c).start()
     total = part[me_y]
     for p in range(1, ny):
         scatter(p).wait_recv()
@@ -90,6 +88,8 @@
 
     for p in range(1, ny):
         gather(p).start()
+    for c in range(chunks):
+        keep(c).start()
     for p in range(1, ny):
         gather(p).wait_recv()
     for p in range(ny):

time: 27.6 us -> 27.6 us (level)
  no operation moved by 1% of the time
where the time goes in v3:
time: 27.6 us; the launch traced here: 27.4 us
  Pallas kernels  26.1 us (95%)
  between operations  1.28 us (5%)
    pallas_call x1, Pallas kernels, summed_gram(): pl.pallas_call(functools.partial(gram_kernel, nx, ny), out_shape=(jax.Sha...  18.4 us
    pallas_call x1, Pallas kernels, project(): pl.pallas_call(project_kernel, out_shape=(jax.ShapeDtypeStruct((count, ro...  7.75 us

profile of v3, /device:TPU:0, one launch (start us, length us, event | category | flops | bytes accessed | tf_op | source)
XLA Modules:
  0.0 27.4 jit_solution(15662179798380101000)
XLA Ops:
  1.3 18.4 %gram.1 = (f32[128,128]{1,0:T(8,128)}, bf16[128,128,128]{2,1,0:T(8,128)(2,1)}) custom-call(bf16[128,128,128]{2,1,0:T(8,128)(2,1)} %data_hbm.1), custom_call_target="tpu_custom_call" | custom-call | tf_op jit(solution)/shard_map/gram/pallas_call | solution.py:112
  19.6 7.7 %project.1 = (bf16[32,128,128]{2,1,0:T(8,128)(2,1)}, f32[32,128]{1,0:T(8,128)}) custom-call(s32[1]{0:T(128)S(6)} %copy.6.rank_ref, f32[128,128]{1,0:T(8,128)} %get-tuple-element.6.gram_ref, f32[1,128]{1,0:T(1,128)} %bitcast.4, f32[32,128]{1,0:T(8,128)} %bitcast.3, bf16[128,128,128]{2,1,0:T(8,128)(2,1)} %get-tuple-element.7.turned_hbm), custom_call_target="tpu_custom_call" | custom-call | tf_op jit(solution)/shard_map/project/pallas_call | solution.py:223
